TPU v7x, 32 devices: a whole 2x2x4 slice. The times are simulated.
32 devices in a mesh: chan: 2 (over x), stn: 16 (over z, y, core).
Axes of the slice: x: 2, y: 2, z: 4, core: 2. Of those that a mesh axis runs over, the one named last changes fastest.
Arguments:
- volts: bfloat16 [2, 128, 38, 3072], P(None, 'stn', 'chan'), may hold values from -6 to 6
- fir: float32 [16, 3072], replicated, may hold values from -0.02734375 to 0.02734375
- gains: float32 [2, 24, 128, 128], P(None, 'chan', 'stn'), may hold values from -4 to 4
- delays: float32 [288, 128], replicated, may hold values from -16 to 16
- subsets: int32 [288, 128], replicated, may hold values from 0 to 127, as said below
- beam_sizes: int32 [288], replicated, may hold values from 1 to 128
- station_ids: int32 [128], replicated, may hold values from 0 to 127, each once
- beam_order: int32 [288], replicated, may hold values from 0 to 287, each once
Outputs:
- beams: bfloat16 [2, 24, 128, 288, 8], P(None, 'chan', None, 'stn')
Inputs may be any that keep to these rules, and one draw needn't show every extreme that they name: Each row of subsets lists every station id once; beam b uses its first beam_sizes[b] entries.
All inputs are finite; a program needn't handle non-finite values.
Results may differ from a plain program's by a relative error of at most 0.0057.
Values may be sent and summed in bfloat16 or wider, within the bound.
A program may use at most 64 MiB of HBM per device.

v0:
```python
import functools
import math

import jax
import jax.numpy as jnp
import numpy as np
from jax import lax
from jax.experimental import pallas as pl
from jax.experimental.pallas import tpu as pltpu
from jax.sharding import PartitionSpec as P

RADIX = 24
SUBLEN = 128
NCH = 3072


full_turn = 2.0 * math.pi


def membership(subsets, beam_sizes):
    beam_count = subsets.shape[0]
    station_count = subsets.shape[1]
    block_count = 8
    per_block = beam_count // block_count
    station_range = jnp.arange(station_count, dtype=jnp.int32)

    def one_block(inputs):
        rows, sizes = inputs
        valid = station_range[None, :] < sizes[:, None]
        listed = rows[:, :, None] == station_range[None, None, :]
        return jnp.any(listed & valid[:, :, None], axis=1).astype(jnp.float32)

    blocked = lax.map(
        one_block,
        (
            subsets.reshape(block_count, per_block, station_count),
            beam_sizes.reshape(block_count, per_block),
        ),
    )
    return blocked.reshape(beam_count, station_count)


def dft_table(length, modulus):
    index = jnp.arange(length)
    angle = (
        full_turn
        * (index[:, None] * jnp.arange(modulus)[None, :] % modulus).astype(jnp.float32)
        / modulus
    )
    return (jnp.cos(angle), jnp.sin(angle))


def finish_transform(twisted_real, twisted_imag):
    highest = lax.Precision.HIGHEST
    cos_table, sin_table = dft_table(SUBLEN, SUBLEN)
    out_real = jnp.einsum("dafs,ac->dcfs", twisted_real, cos_table, precision=highest) + jnp.einsum(
        "dafs,ac->dcfs", twisted_imag, sin_table, precision=highest
    )
    out_imag = jnp.einsum("dafs,ac->dcfs", twisted_imag, cos_table, precision=highest) - jnp.einsum(
        "dafs,ac->dcfs", twisted_real, sin_table, precision=highest
    )
    return jnp.stack([out_real, out_imag]).astype(jnp.bfloat16)


def body(volts, fir, gains, delays, subsets, beam_sizes, station_ids, beam_order):
    highest = lax.Precision.HIGHEST
    taps = fir.shape[0]
    stn_dev = volts.shape[1]
    frames_dev = volts.shape[2] - taps + 1
    filtered = jnp.zeros((2, stn_dev, frames_dev, NCH), jnp.float32)
    for tap_index in range(taps):
        filtered = filtered + fir[tap_index] * volts[
            :, :, tap_index : tap_index + frames_dev, :
        ].astype(jnp.float32)
    real_part = filtered[0].reshape(stn_dev, frames_dev, RADIX, SUBLEN)
    imag_part = filtered[1].reshape(stn_dev, frames_dev, RADIX, SUBLEN)
    first_cos, first_sin = dft_table(RADIX, RADIX)
    section_real = jnp.einsum(
        "sfba,bd->dafs", real_part, first_cos, precision=highest
    ) + jnp.einsum("sfba,bd->dafs", imag_part, first_sin, precision=highest)
    section_imag = jnp.einsum(
        "sfba,bd->dafs", imag_part, first_cos, precision=highest
    ) - jnp.einsum("sfba,bd->dafs", real_part, first_sin, precision=highest)
    twist_angle = (
        full_turn
        * (jnp.arange(RADIX)[:, None] * jnp.arange(SUBLEN)[None, :] % NCH).astype(jnp.float32)
        / NCH
    )
    twist_cos = jnp.cos(twist_angle)[:, :, None, None]
    twist_sin = jnp.sin(twist_angle)[:, :, None, None]
    twisted_real = section_real * twist_cos + section_imag * twist_sin
    twisted_imag = section_imag * twist_cos - section_real * twist_sin
    spectra = finish_transform(twisted_real, twisted_imag).reshape(
        2, RADIX, SUBLEN, frames_dev * stn_dev
    )
    turned = lax.all_to_all(spectra, "chan", split_axis=1, concat_axis=3, tiled=True)
    local_data = lax.all_to_all(turned, "stn", split_axis=2, concat_axis=3, tiled=True)
    radix_local = local_data.shape[1]
    sub_local = local_data.shape[2]
    groups = lax.axis_size("stn")
    frames_all = local_data.shape[3] // (groups * stn_dev)
    grouped = local_data.reshape(2, radix_local, sub_local, groups, frames_all, stn_dev)
    beam_count = subsets.shape[0]
    member = membership(subsets, beam_sizes)
    weight_mask = (
        member[:, station_ids][beam_order]
        * lax.rsqrt(beam_sizes[beam_order].astype(jnp.float32))[:, None]
    )
    delay_rows = delays[:, station_ids][beam_order]
    gain_rows = jnp.take(gains, station_ids, axis=3)
    radix_index = lax.axis_index("chan") * radix_local + jnp.arange(radix_local)
    sub_index = lax.axis_index("stn") * sub_local + jnp.arange(sub_local)
    chan_index = (RADIX * sub_index[None, :] + radix_index[:, None]).astype(jnp.float32)
    angle = (full_turn * chan_index)[:, :, None, None] * delay_rows[None, None] / NCH
    cosine = jnp.cos(angle)
    sine = jnp.sin(angle)
    gain_real = gain_rows[0][:, :, None, :]
    gain_imag = gain_rows[1][:, :, None, :]
    shape_split = (radix_local, sub_local, beam_count, groups, stn_dev)
    weight_real = (
        ((gain_real * cosine + gain_imag * sine) * weight_mask[None, None])
        .astype(jnp.bfloat16)
        .reshape(shape_split)
    )
    weight_imag = (
        ((gain_imag * cosine - gain_real * sine) * weight_mask[None, None])
        .astype(jnp.bfloat16)
        .reshape(shape_split)
    )
    form = "dcbgs,dcgts->dcbt"
    data_real = grouped[0]
    data_imag = grouped[1]
    beam_real = jnp.einsum(
        form, weight_real, data_real, preferred_element_type=jnp.float32
    ) - jnp.einsum(form, weight_imag, data_imag, preferred_element_type=jnp.float32)
    beam_imag = jnp.einsum(
        form, weight_real, data_imag, preferred_element_type=jnp.float32
    ) + jnp.einsum(form, weight_imag, data_real, preferred_element_type=jnp.float32)
    formed = jnp.stack([beam_real, beam_imag]).astype(jnp.bfloat16)
    return lax.all_to_all(formed, "stn", split_axis=3, concat_axis=2, tiled=True)


LANES = 128
ROWS = 8
VMEM_BYTES = 62 * 1024 * 1024


def small_factor(length):
    for factor in (2, 3, 5, 7):
        if length % factor == 0:
            return factor
    return length


def rotate(value, turn):
    real, imag = value
    turn = turn % 1.0
    if turn == 0.0:
        return value
    if turn == 0.5:
        return (-real, -imag)
    if turn == 0.25:
        return (imag, -real)
    if turn == 0.75:
        return (-imag, real)
    cosine, sine = math.cos(full_turn * turn), math.sin(full_turn * turn)
    return (real * cosine + imag * sine, imag * cosine - real * sine)


def short_transform(values):
    length = len(values)
    if length == 1:
        return values
    radix = small_factor(length)
    inner = length // radix
    parts = [short_transform(values[offset::radix]) for offset in range(radix)]
    out = [None] * length
    for low in range(inner):
        terms = [rotate(parts[j][low], j * low / length) for j in range(radix)]
        for high in range(radix):
            total = terms[0]
            for j in range(1, radix):
                turned = rotate(terms[j], j * high / radix)
                total = (total[0] + turned[0], total[1] + turned[1])
            out[low + inner * high] = total
    return out


def swap_granules(tiles, width):
    count = len(tiles)
    lane = lax.broadcasted_iota(jnp.int32, tiles[0].shape, 1)
    bit = 1
    while bit < count:
        shift = bit * width
        low_side = (lane // shift) % 2 == 0
        fresh = list(tiles)
        for index in range(count):
            if index & bit == 0:
                first, second = tiles[index], tiles[index | bit]
                fresh[index] = jnp.where(low_side, first, pltpu.roll(second, shift, 1))
                fresh[index | bit] = jnp.where(
                    low_side, pltpu.roll(first, LANES - shift, 1), second
                )
        tiles = fresh
        bit *= 2
    return tiles


def transform_volts(dims, volts_ref, fir_ref, cos_ref, sin_ref, table_ref, out_ref, kept, rows):
    taps, frames, radix, chan_dev, stn_groups, blocks = dims
    granule = LANES // (2 * frames)

    def filter_tile(b, carry):
        spot = pl.ds(pl.multiple_of(b * LANES, LANES), LANES)
        for part in range(2):
            block = volts_ref[part, :, :, spot].astype(jnp.float32)
            for frame in range(frames):
                total = fir_ref[0:1, spot] * block[frame]
                for tap in range(1, taps):
                    total = total + fir_ref[tap : tap + 1, spot] * block[frame + tap]
                kept[part, frame, b] = total
        return carry

    lax.fori_loop(0, radix, filter_tile, 0)
    pairs = radix // 2
    for frame in range(frames):
        section = short_transform(
            [(kept[0, frame, b], kept[1, frame, b]) for b in range(radix)]
        )
        for d in range(radix):
            real, imag = section[d]
            cosine, sine = cos_ref[d : d + 1, :], sin_ref[d : d + 1, :]
            start = (((d % 2) * frames + frame) * pairs + d // 2) * ROWS
            rows[start : start + ROWS, :LANES] = real * cosine + imag * sine
            rows[start : start + ROWS, LANES:] = imag * cosine - real * sine
    spectra = jnp.dot(
        rows[...],
        table_ref[...],
        preferred_element_type=jnp.float32,
        precision=lax.Precision.HIGHEST,
    )
    size = pairs * ROWS
    share = size // chan_dev
    part = share // blocks
    per_tile = LANES // granule
    for high in range(stn_groups // per_tile):
        tiles = swap_granules(
            [
                spectra[ef * size : (ef + 1) * size, high * LANES : (high + 1) * LANES]
                for ef in range(2 * frames)
            ],
            granule,
        )
        for low in range(per_tile):
            for chan in range(chan_dev):
                for step in range(blocks):
                    start = chan * share + step * part
                    out_ref[step, chan * stn_groups + high * per_tile + low] = tiles[low][
                        start : start + part
                    ].astype(jnp.bfloat16)


def one_hot(ids, size):
    rows = lax.broadcasted_iota(jnp.int32, (size, ids.shape[1]), 0)
    return jnp.where(rows == ids, 1.0, 0.0)


def exact(left, right, transposed=False):
    contract = ((0 if transposed else 1,), (0,))
    return lax.dot_general(
        left,
        right,
        (contract, ((), ())),
        precision=lax.Precision.HIGHEST,
        preferred_element_type=jnp.float32,
    )


def whole_kernel(
    dims,
    volts_in,
    fir_in,
    cos_in,
    sin_in,
    table_in,
    gain_in,
    delay_in,
    subset_in,
    ids_in,
    order_in,
    out_ref,
    volts_ref,
    fir_ref,
    cos_ref,
    sin_ref,
    table_ref,
    gain_ref,
    delay_ref,
    subset_ref,
    ids_ref,
    order_ref,
    load_sems,
    kept,
    rows,
    piece_ref,
    data,
    listed,
    member,
    picked,
    delay_rows,
    gain_rows,
    state,
    turns,
    weights,
    rhs,
    formed,
    landed,
    spread,
    in_send,
    in_recv,
    out_send,
    out_recv,
):
    group, subs, chan_dev, stn_groups, frames_all, radix_local = dims
    beams, stations = delay_ref.shape
    radix = radix_local * chan_dev
    channels = fir_ref.shape[1]
    taps = fir_ref.shape[0]
    blocks = radix_local // group
    per_dest = beams // stn_groups
    rows_each = group * per_dest
    devices = chan_dev * stn_groups
    row_block = 2 * ROWS
    my_chan, my_stn = lax.axis_index("chan"), lax.axis_index("stn")
    me = my_chan * stn_groups + my_stn

    def place(peer):
        return {"chan": peer // stn_groups, "stn": peer % stn_groups}

    barrier = pltpu.get_barrier_semaphore()

    def greet(offset, carry):
        peer = (me + offset) % devices
        pl.semaphore_signal(
            barrier, inc=1, device_id=place(peer), device_id_type=pl.DeviceIdType.MESH
        )
        return carry

    loads = [
        pltpu.make_async_copy(source, target, load_sems.at[index])
        for index, (source, target) in enumerate(
            (
                (volts_in, volts_ref),
                (fir_in, fir_ref),
                (cos_in, cos_ref),
                (sin_in, sin_ref),
                (table_in, table_ref),
                (order_in, order_ref),
                (subset_in, subset_ref),
                (ids_in, ids_ref),
                (delay_in, delay_ref),
                (gain_in, gain_ref),
            )
        )
    ]
    for load in loads:
        load.start()
    lax.fori_loop(1, devices, greet, 0)
    for load in loads:
        load.wait()
    transform_volts(
        (taps, frames_all // chan_dev, radix, chan_dev, stn_groups, blocks),
        volts_ref, fir_ref, cos_ref, sin_ref, table_ref, piece_ref, kept, rows,
    )
    ordered = one_hot(order_ref[1:2, :], beams)
    ordered_narrow = ordered.astype(jnp.bfloat16)
    sizes = jnp.dot(
        jnp.broadcast_to(order_ref[0:1, :], (ROWS, beams)).astype(jnp.float32).astype(jnp.bfloat16),
        ordered_narrow,
        preferred_element_type=jnp.float32,
    )[0:1, :]
    entries = lax.dot_general(
        subset_ref[...].astype(jnp.float32).astype(jnp.bfloat16),
        ordered_narrow,
        (((0,), (0,)), ((), ())),
        preferred_element_type=jnp.float32,
    )
    position = lax.broadcasted_iota(jnp.int32, (stations, beams), 0).astype(jnp.float32)
    listed[...] = jnp.where(position < sizes, entries, -1.0)
    scale = lax.rsqrt(sizes)
    pl.semaphore_wait(barrier, devices - 1)

    def piece_copy(step, peer, slot):
        return pltpu.make_async_remote_copy(
            src_ref=piece_ref.at[step, peer],
            dst_ref=data.at[step, slot],
            send_sem=in_send.at[step, peer],
            recv_sem=in_recv.at[step, slot],
            device_id=place(peer),
            device_id_type=pl.DeviceIdType.MESH,
        )

    def send_pieces(step, carry):
        def send_piece(offset, inner):
            piece_copy(step, (me + offset) % devices, me).start()
            return inner

        lax.fori_loop(1, devices, send_piece, 0)
        data[step, me] = piece_ref[step, me]
        return carry

    lax.fori_loop(0, blocks, send_pieces, 0)

    block = 4 * ROWS
    for start in range(0, stations, block):
        ids = (lax.broadcasted_iota(jnp.int32, (block, beams), 0) + start).astype(jnp.float32)

        def look(p, total):
            entries = listed[pl.ds(pl.multiple_of(p * ROWS, ROWS), ROWS), :]
            for row in range(ROWS):
                total = jnp.where(entries[row : row + 1, :] == ids, 1.0, total)
            return total

        found = lax.fori_loop(
            0, stations // ROWS, look, jnp.zeros((block, beams), jnp.float32)
        )
        member[start : start + block, :] = found * scale
    station_pick = one_hot(ids_ref[...], stations)
    picked[...] = exact(member[...], station_pick, transposed=True)
    delay_rows[...] = exact(ordered, exact(delay_ref[...], station_pick), transposed=True)
    gain_rows[...] = exact(gain_ref[...], station_pick)
    first_chan = (radix * subs * my_stn + radix_local * my_chan).astype(jnp.float32)

    def phase(delay, step):
        turn = delay * (step / channels)
        angle = (turn - jnp.round(turn)) * full_turn
        return jnp.cos(angle), jnp.sin(angle)

    def begin(index, carry):
        spot = pl.ds(pl.multiple_of(index * row_block, row_block), row_block)
        delay, mask = delay_rows[spot, :], picked[spot, :]
        cosine, sine = phase(delay, first_chan)
        jump_cos, jump_sin = phase(delay, float(radix))
        turns[0, spot, :], turns[1, spot, :] = phase(delay, 1.0)
        real, imag = cosine * mask, -sine * mask
        for sub in range(subs):
            state[0, sub, spot, :] = real
            state[1, sub, spot, :] = imag
            real, imag = real * jump_cos + imag * jump_sin, imag * jump_cos - real * jump_sin
        return carry

    lax.fori_loop(0, beams // row_block, begin, 0)

    def weigh(index, carry):
        spot = pl.ds(pl.multiple_of(index * row_block, row_block), row_block)
        cosine, sine = turns[0, spot, :], turns[1, spot, :]
        for sub in range(subs):
            at = 2 * stations * sub
            real, imag = state[0, sub, spot, :], state[1, sub, spot, :]
            for local in range(group):
                weights[local, spot, at : at + stations] = real.astype(jnp.bfloat16)
                weights[local, spot, at + stations : at + 2 * stations] = imag.astype(jnp.bfloat16)
                real, imag = real * cosine + imag * sine, imag * cosine - real * sine
            state[0, sub, spot, :] = real
            state[1, sub, spot, :] = imag
        return carry

    lax.fori_loop(0, beams // row_block, weigh, 0)

    lane = lax.broadcasted_iota(jnp.int32, (stations, LANES), 1)
    is_real = (lane // subs) % 2 == 0
    sub_of = lane % subs
    half = LANES // chan_dev

    def exchange(value):
        return jnp.where(
            is_real, pltpu.roll(value, LANES - subs, 1), pltpu.roll(value, subs, 1)
        )

    def beam_copy(step, stn, slot):
        return pltpu.make_async_remote_copy(
            src_ref=formed.at[step, stn],
            dst_ref=landed.at[step, slot],
            send_sem=out_send.at[step, stn],
            recv_sem=out_recv.at[step, slot],
            device_id={"chan": my_chan, "stn": stn},
            device_id_type=pl.DeviceIdType.MESH,
        )

    def form(step, carry):
        def take_piece(offset, inner):
            peer = (me + offset) % devices
            piece_copy(step, peer, peer).wait_recv()
            return inner

        lax.fori_loop(1, devices, take_piece, 0)
        for local in range(group):
            at = (local // 2) * ROWS
            blocks_in = [
                data[step, c * stn_groups : (c + 1) * stn_groups, at : at + ROWS, :]
                .astype(jnp.float32)
                .reshape(stations, LANES)
                for c in range(2)
            ]
            if local % 2 == 0:
                both = jnp.where(lane < half, blocks_in[0], pltpu.roll(blocks_in[1], half, 1))
            else:
                both = jnp.where(lane < half, pltpu.roll(blocks_in[0], half, 1), blocks_in[1])
            gain_real, gain_imag = (
                jnp.concatenate(
                    [
                        gain_rows[
                            pl.ds(
                                pl.multiple_of(
                                    (part * radix_local + step * group + local) * subs, subs
                                ),
                                subs,
                            ),
                            :,
                        ]
                    ]
                    * (LANES // subs),
                    axis=0,
                ).T
                for part in range(2)
            )
            top = gain_real * both + jnp.where(is_real, -gain_imag, gain_imag) * exchange(both)
            bottom = exchange(top)
            bottom = jnp.where(is_real, -bottom, bottom)
            for sub in range(subs):
                at = 2 * stations * sub
                chosen = sub_of == sub
                rhs[at : at + stations, :] = jnp.where(chosen, top, 0.0).astype(jnp.bfloat16)
                rhs[at + stations : at + 2 * stations, :] = jnp.where(
                    chosen, bottom, 0.0
                ).astype(jnp.bfloat16)
            result = jnp.dot(
                weights[local], rhs[...], preferred_element_type=jnp.float32
            )
            for dest in range(stn_groups):
                formed[step, dest, local * per_dest : (local + 1) * per_dest, :] = result[
                    dest * per_dest : (dest + 1) * per_dest
                ].astype(jnp.bfloat16)

        def send_beams(offset, inner):
            beam_copy(step, (my_stn + offset) % stn_groups, my_stn).start()
            return inner

        lax.fori_loop(1, stn_groups, send_beams, 0)
        landed[step, my_stn] = formed[step, my_stn]

        @pl.when(step < blocks - 1)
        def _():
            lax.fori_loop(0, beams // row_block, weigh, 0)

        return carry

    lax.fori_loop(0, blocks, form, 0)

    def finish(step, carry):
        def take_beams(offset, inner):
            stn = (my_stn + offset) % stn_groups
            beam_copy(step, stn, stn).wait_recv()
            return inner

        lax.fori_loop(1, stn_groups, take_beams, 0)
        tiles = swap_granules(
            [landed[step, source].astype(jnp.float32) for source in range(stn_groups)],
            LANES // stn_groups,
        )
        for part in range(2):
            for t in range(frames_all):
                spread[pl.ds(t, rows_each, stride=frames_all), :] = tiles[2 * t + part]
            out_ref[part, step] = spread[: rows_each * frames_all, :].astype(jnp.bfloat16)
        return carry

    lax.fori_loop(0, blocks, finish, 0)

    def settle_pieces(step, carry):
        def settle(offset, inner):
            piece_copy(step, (me + offset) % devices, me).wait_send()
            return inner

        lax.fori_loop(1, devices, settle, 0)
        return carry

    lax.fori_loop(0, blocks, settle_pieces, 0)

    def settle_beams(step, carry):
        def settle(offset, inner):
            beam_copy(step, (my_stn + offset) % stn_groups, my_stn).wait_send()
            return inner

        lax.fori_loop(1, stn_groups, settle, 0)
        return carry

    lax.fori_loop(0, blocks, settle_beams, 0)


def fused_body(group, volts, fir, gains, delays, subsets, beam_sizes, station_ids, beam_order):
    f32, bf16 = jnp.float32, jnp.bfloat16
    taps = fir.shape[0]
    stn_dev = volts.shape[1]
    frames = volts.shape[2] - taps + 1
    chan_dev = lax.axis_size("chan")
    groups = lax.axis_size("stn")
    radix_local, subs, stations = gains.shape[1:]
    beams = delays.shape[0]
    radix = radix_local * chan_dev
    channels = fir.shape[1]
    sublen = channels // radix
    pairs = radix_local // 2
    per_dest = beams // groups
    frames_all = frames * chan_dev

    turn = np.arange(radix)[:, None] * np.arange(sublen)[None, :] * (2 * np.pi / channels)
    index = np.arange(sublen)
    angle = (index[:, None] * index[None, :] % sublen) * (2 * np.pi / sublen)
    cosine, sine = np.cos(angle), np.sin(angle)
    table = np.stack([np.stack([cosine, -sine], 1), np.stack([sine, cosine], 1)])
    table = table.reshape(2 * sublen, 2, groups, subs).transpose(0, 2, 1, 3)
    table = table.reshape(2 * sublen, 2 * sublen).astype(np.float32)

    blocks = radix_local // group
    rows_each = group * per_dest
    devices = chan_dev * groups
    operands = (
        volts.transpose(0, 2, 1, 3),
        fir,
        jnp.asarray(np.cos(turn), f32),
        jnp.asarray(np.sin(turn), f32),
        jnp.asarray(table),
        gains.reshape(2 * radix_local * subs, stations),
        delays,
        subsets,
        station_ids[None, :],
        jnp.stack([beam_sizes, beam_order]),
    )
    done = pl.pallas_call(
        functools.partial(whole_kernel, (group, subs, chan_dev, groups, frames_all, radix_local)),
        in_specs=[pl.BlockSpec(memory_space=pltpu.HBM)] * len(operands),
        out_specs=pl.BlockSpec(memory_space=pltpu.VMEM),
        out_shape=jax.ShapeDtypeStruct((2, blocks, rows_each * frames_all, LANES), bf16),
        scratch_shapes=[pltpu.VMEM(value.shape, value.dtype) for value in operands]
        + [
            pltpu.SemaphoreType.DMA((len(operands),)),
            pltpu.VMEM((2, frames, radix, stn_dev, LANES), f32),
            pltpu.VMEM((radix * frames * stn_dev, 2 * LANES), f32),
            pltpu.VMEM((blocks, devices, group // 2 * ROWS, LANES), bf16),
            pltpu.VMEM((blocks, devices, group // 2 * ROWS, LANES), bf16),
            pltpu.VMEM((stations, beams), f32),
            pltpu.VMEM((stations, beams), f32),
            pltpu.VMEM((beams, stations), f32),
            pltpu.VMEM((beams, stations), f32),
            pltpu.VMEM((2 * radix_local * subs, stations), f32),
            pltpu.VMEM((2, subs, beams, stations), f32),
            pltpu.VMEM((2, beams, stations), f32),
            pltpu.VMEM((group, beams, 2 * stations * subs), bf16),
            pltpu.VMEM((2 * stations * subs, LANES), bf16),
            pltpu.VMEM((blocks, groups, rows_each, LANES), bf16),
            pltpu.VMEM((blocks, groups, rows_each, LANES), bf16),
            pltpu.VMEM((rows_each * frames_all, LANES), f32),
            pltpu.SemaphoreType.DMA((blocks, devices)),
            pltpu.SemaphoreType.DMA((blocks, devices)),
            pltpu.SemaphoreType.DMA((blocks, groups)),
            pltpu.SemaphoreType.DMA((blocks, groups)),
        ],
        compiler_params=pltpu.CompilerParams(
            collective_id=0, has_side_effects=True, vmem_limit_bytes=VMEM_BYTES
        ),
        name="whole",
    )(*operands)
    done = done.reshape(2, radix_local, per_dest, frames_all, sublen)
    return done.transpose(0, 1, 4, 2, 3)


def group_size(mesh, volts, fir, gains, delays):
    chan_dev, stn_groups = mesh.shape["chan"], mesh.shape["stn"]
    radix_local, subs = gains.shape[1] // chan_dev, gains.shape[2] // stn_groups
    stations, beams = gains.shape[3], delays.shape[0]
    frames = volts.shape[2] // chan_dev - fir.shape[0] + 1
    fits = (
        chan_dev == 2
        and volts.shape[1] // stn_groups == ROWS
        and gains.shape[2] == LANES
        and stations == LANES
        and subs * stn_groups == LANES
        and subs * 2 * frames * chan_dev == LANES
        and stn_groups == 2 * frames * chan_dev
        and beams % (2 * ROWS) == 0
        and radix_local % 2 == 0
    )
    if fits:
        for group in range(2, radix_local + 1, 2):
            if radix_local % group == 0 and group * (beams // stn_groups) % ROWS == 0:
                return group
    return 0


def solution(mesh):
    placed = (
        P(None, "stn", "chan", None),
        P(),
        P(None, "chan", "stn", None),
        P(),
        P(),
        P(),
        P(),
        P(),
    )

    def run(volts, fir, gains, delays, *others):
        group = group_size(mesh, volts, fir, gains, delays)
        return jax.shard_map(
            functools.partial(fused_body, group) if group else body,
            mesh=mesh,
            in_specs=placed,
            out_specs=P(None, "chan", None, "stn", None),
            check_vma=False,
        )(volts, fir, gains, delays, *others)

    return run
```

profile of v0, /device:TPU:0, one launch (start us, length us, event | category | flops | bytes accessed | tf_op | source)
XLA Modules:
  0.0 48.5 jit_solution(3570764381561907697)
XLA Ops:
  0.0 0.7 %stack.9 = s32[1,288]{1,0:T(1,128)S(1)} reshape(s32[288]{0:T(512)} %param.16) | data formatting | bytes 2304 | tf_op jit(solution)/shard_map/stack | solution.py:637
  0.7 0.7 %stack.10 = s32[1,288]{1,0:T(1,128)S(1)} reshape(s32[288]{0:T(512)} %param.18) | data formatting | bytes 2304 | tf_op jit(solution)/shard_map/stack | solution.py:637
  1.4 0.6 %pad_add_fusion.order_in = s32[2,288]{1,0:T(2,128)} fusion(s32[1,288]{1,0:T(1,128)S(1)} %stack.10, s32[1,288]{1,0:T(1,128)S(1)} %stack.9), kind=kLoop, calls=%fused_computation | loop fusion | flops 576 | bytes 4608 | tf_op jit(solution)/shard_map/stack | solution.py:637
  2.0 44.4 %whole.1 = bf16[2,3,576,128]{3,2,1,0:T(8,128)(2,1)} custom-call(bf16[2,19,8,3072]{3,2,1,0:T(8,128)(2,1)} %bitcast.7, f32[16,3072]{1,0:T(8,128)} %fir_in.1, f32[24,128]{1,0:T(8,128)} %constant.6.clone.cos_in, f32[24,128]{1,0:T(8,128)} %constant.7.clone.sin_in, f32[256,256]{1,0:T(8,128)} %constant.8.clone.table_in, f32[192,128]{1,0:T(8,128)} %bitcast.8, ...), custom_call_target="tpu_custom_call" | custom-call | tf_op jit(solution)/shard_map/whole/pallas_call | solution.py:639
  46.4 2.1 %copy.13 = bf16[2,12,128,18,8]{2,4,3,1,0:T(8,128)(2,1)} copy(bf16[2,12,128,18,8]{2,4,3,1,0:T(8,128)(2,1)} %bitcast.6) | data formatting | bytes 1769472
where the time goes:
time: 48.7 us; the launch traced here: 48.5 us
  Pallas kernels  44.4 us (91%)
  local copies, waits for them, and re-layouts  3.5 us (7%)
  other arithmetic  0.59 us (1%)
    pallas_call x1, Pallas kernels, fused_body(): pl.pallas_call(functools.partial(whole_kernel, (group, subs, chan_dev, gr...  44.4 us
    unnamed x1, local copies, waits for them, and re-layouts  2.14 us
    another operation x2, local copies, waits for them, and re-layouts, fused_body(): jnp.stack([beam_sizes, beam_order])  1.37 us

commit v1 on v0

--- a/solution.py
+++ b/solution.py
@@ -287,6 +287,7 @@
     delay_in,
     subset_in,
     ids_in,
+    sizes_in,
     order_in,
     out_ref,
     volts_ref,
@@ -298,6 +299,7 @@
     delay_ref,
     subset_ref,
     ids_ref,
+    sizes_ref,
     order_ref,
     load_sems,
     kept,
@@ -355,6 +357,7 @@
                 (cos_in, cos_ref),
                 (sin_in, sin_ref),
                 (table_in, table_ref),
+                (sizes_in, sizes_ref),
                 (order_in, order_ref),
                 (subset_in, subset_ref),
                 (ids_in, ids_ref),
@@ -372,10 +375,10 @@
         (taps, frames_all // chan_dev, radix, chan_dev, stn_groups, blocks),
         volts_ref, fir_ref, cos_ref, sin_ref, table_ref, piece_ref, kept, rows,
     )
-    ordered = one_hot(order_ref[1:2, :], beams)
+    ordered = one_hot(order_ref[...][None, :], beams)
     ordered_narrow = ordered.astype(jnp.bfloat16)
     sizes = jnp.dot(
-        jnp.broadcast_to(order_ref[0:1, :], (ROWS, beams)).astype(jnp.float32).astype(jnp.bfloat16),
+        jnp.broadcast_to(sizes_ref[...][None, :], (ROWS, beams)).astype(jnp.float32).astype(jnp.bfloat16),
         ordered_narrow,
         preferred_element_type=jnp.float32,
     )[0:1, :]
@@ -388,29 +391,6 @@
     position = lax.broadcasted_iota(jnp.int32, (stations, beams), 0).astype(jnp.float32)
     listed[...] = jnp.where(position < sizes, entries, -1.0)
     scale = lax.rsqrt(sizes)
-    pl.semaphore_wait(barrier, devices - 1)
-
-    def piece_copy(step, peer, slot):
-        return pltpu.make_async_remote_copy(
-            src_ref=piece_ref.at[step, peer],
-            dst_ref=data.at[step, slot],
-            send_sem=in_send.at[step, peer],
-            recv_sem=in_recv.at[step, slot],
-            device_id=place(peer),
-            device_id_type=pl.DeviceIdType.MESH,
-        )
-
-    def send_pieces(step, carry):
-        def send_piece(offset, inner):
-            piece_copy(step, (me + offset) % devices, me).start()
-            return inner
-
-        lax.fori_loop(1, devices, send_piece, 0)
-        data[step, me] = piece_ref[step, me]
-        return carry
-
-    lax.fori_loop(0, blocks, send_pieces, 0)
-
     block = 4 * ROWS
     for start in range(0, stations, block):
         ids = (lax.broadcasted_iota(jnp.int32, (block, beams), 0) + start).astype(jnp.float32)
@@ -425,7 +405,7 @@
             0, stations // ROWS, look, jnp.zeros((block, beams), jnp.float32)
         )
         member[start : start + block, :] = found * scale
-    station_pick = one_hot(ids_ref[...], stations)
+    station_pick = one_hot(ids_ref[...][None, :], stations)
     picked[...] = exact(member[...], station_pick, transposed=True)
     delay_rows[...] = exact(ordered, exact(delay_ref[...], station_pick), transposed=True)
     gain_rows[...] = exact(gain_ref[...], station_pick)
@@ -450,6 +430,28 @@
         return carry
 
     lax.fori_loop(0, beams // row_block, begin, 0)
+    pl.semaphore_wait(barrier, devices - 1)
+
+    def piece_copy(step, peer, slot):
+        return pltpu.make_async_remote_copy(
+            src_ref=piece_ref.at[step, peer],
+            dst_ref=data.at[step, slot],
+            send_sem=in_send.at[step, peer],
+            recv_sem=in_recv.at[step, slot],
+            device_id=place(peer),
+            device_id_type=pl.DeviceIdType.MESH,
+        )
+
+    def send_pieces(step, carry):
+        def send_piece(offset, inner):
+            piece_copy(step, (me + offset) % devices, me).start()
+            return inner
+
+        lax.fori_loop(1, devices, send_piece, 0)
+        data[step, me] = piece_ref[step, me]
+        return carry
+
+    lax.fori_loop(0, blocks, send_pieces, 0)
 
     def weigh(index, carry):
         spot = pl.ds(pl.multiple_of(index * row_block, row_block), row_block)
@@ -633,14 +635,15 @@
         gains.reshape(2 * radix_local * subs, stations),
         delays,
         subsets,
-        station_ids[None, :],
-        jnp.stack([beam_sizes, beam_order]),
+        station_ids,
+        beam_sizes,
+        beam_order,
     )
     done = pl.pallas_call(
         functools.partial(whole_kernel, (group, subs, chan_dev, groups, frames_all, radix_local)),
         in_specs=[pl.BlockSpec(memory_space=pltpu.HBM)] * len(operands),
         out_specs=pl.BlockSpec(memory_space=pltpu.VMEM),
-        out_shape=jax.ShapeDtypeStruct((2, blocks, rows_each * frames_all, LANES), bf16),
+        out_shape=pltpu.VMEM((2, blocks, rows_each * frames_all, LANES), bf16),
         scratch_shapes=[pltpu.VMEM(value.shape, value.dtype) for value in operands]
         + [
             pltpu.SemaphoreType.DMA((len(operands),)),

time: 48.7 us -> 46.9 us (0.963)
  local copies, waits for them, and re-layouts: 3.5 us -> 0.91 us
  Pallas kernels: 44.4 us -> 45.9 us
  other arithmetic: 0.59 us -> 0 us
    pallas_call x1, Pallas kernels: 44.4 us -> 45.9 us  [fused_body(): pl.pallas_call(functools.partial(whole_kernel, (group, subs, chan_dev, gr...]
    another operation x2 -> x0, local copies, waits for them, and re-layouts: 1.37 us -> none  [fused_body(): jnp.stack([beam_sizes, beam_order])]
    unnamed x1, local copies, waits for them, and re-layouts: 2.14 us -> 0.91 us
    another operation x1 -> x0, other arithmetic: 0.59 us -> none  [fused_body(): jnp.stack([beam_sizes, beam_order])]
where the time goes in v1:
time: 46.9 us; the launch traced here: 46.8 us
  Pallas kernels  45.9 us (98%)
  local copies, waits for them, and re-layouts  0.91 us (2%)
    pallas_call x1, Pallas kernels, fused_body(): pl.pallas_call(functools.partial(whole_kernel, (group, subs, chan_dev, gr...  45.9 us

profile of v1, /device:TPU:0, one launch (start us, length us, event | category | flops | bytes accessed | tf_op | source)
XLA Modules:
  0.0 46.8 jit_solution(7958078665630993729)
XLA Ops:
  0.0 45.9 %whole.1 = bf16[2,3,576,128]{3,2,1,0:T(8,128)(2,1)S(1)} custom-call(bf16[2,19,8,3072]{3,2,1,0:T(8,128)(2,1)} %bitcast.6, f32[16,3072]{1,0:T(8,128)} %fir_in.1, f32[24,128]{1,0:T(8,128)} %constant.6.clone.cos_in, f32[24,128]{1,0:T(8,128)} %constant.7.clone.sin_in, f32[256,256]{1,0:T(8,128)} %constant.8.clone.table_in, f32[192,128]{1,0:T(8,128)} %bitcast.7, ...), custom_call_target="tpu_custom_call" | custom-call | tf_op jit(solution)/shard_map/whole/pallas_call | solution.py:642
  45.9 0.9 %copy.13 = bf16[2,12,128,18,8]{2,4,3,1,0:T(8,128)(2,1)} copy(bf16[2,12,128,18,8]{2,4,3,1,0:T(8,128)(2,1)S(1)} %bitcast.5) | data formatting | bytes 1769472

commit v2 on v1

--- a/solution.py
+++ b/solution.py
@@ -262,16 +262,23 @@
 
 def one_hot(ids, size):
     rows = lax.broadcasted_iota(jnp.int32, (size, ids.shape[1]), 0)
-    return jnp.where(rows == ids, 1.0, 0.0)
-
-
-def exact(left, right, transposed=False):
-    contract = ((0 if transposed else 1,), (0,))
+    return jnp.where(rows == ids, 1.0, 0.0).astype(jnp.bfloat16)
+
+
+def split(value):
+    parts = []
+    for _ in range(2):
+        part = value.astype(jnp.bfloat16)
+        parts.append(part)
+        value = value - part.astype(jnp.float32)
+    return parts + [value.astype(jnp.bfloat16)]
+
+
+def pick(value, chosen, left=0):
     return lax.dot_general(
-        left,
-        right,
-        (contract, ((), ())),
-        precision=lax.Precision.HIGHEST,
+        jnp.concatenate(split(value), axis=left),
+        jnp.concatenate([chosen] * 3, axis=0),
+        (((left,), (0,)), ((), ())),
         preferred_element_type=jnp.float32,
     )
 
@@ -376,15 +383,14 @@
         volts_ref, fir_ref, cos_ref, sin_ref, table_ref, piece_ref, kept, rows,
     )
     ordered = one_hot(order_ref[...][None, :], beams)
-    ordered_narrow = ordered.astype(jnp.bfloat16)
     sizes = jnp.dot(
         jnp.broadcast_to(sizes_ref[...][None, :], (ROWS, beams)).astype(jnp.float32).astype(jnp.bfloat16),
-        ordered_narrow,
+        ordered,
         preferred_element_type=jnp.float32,
     )[0:1, :]
     entries = lax.dot_general(
         subset_ref[...].astype(jnp.float32).astype(jnp.bfloat16),
-        ordered_narrow,
+        ordered,
         (((0,), (0,)), ((), ())),
         preferred_element_type=jnp.float32,
     )
@@ -406,9 +412,32 @@
         )
         member[start : start + block, :] = found * scale
     station_pick = one_hot(ids_ref[...][None, :], stations)
-    picked[...] = exact(member[...], station_pick, transposed=True)
-    delay_rows[...] = exact(ordered, exact(delay_ref[...], station_pick), transposed=True)
-    gain_rows[...] = exact(gain_ref[...], station_pick)
+    picked[...] = pick(member[...], station_pick)
+    delay_rows[...] = pick(pick(delay_ref[...], ordered), station_pick)
+    gain_rows[...] = pick(gain_ref[...], station_pick, left=1)
+    pl.semaphore_wait(barrier, devices - 1)
+
+    def piece_copy(step, peer, slot):
+        return pltpu.make_async_remote_copy(
+            src_ref=piece_ref.at[step, peer],
+            dst_ref=data.at[step, slot],
+            send_sem=in_send.at[step, peer],
+            recv_sem=in_recv.at[step, slot],
+            device_id=place(peer),
+            device_id_type=pl.DeviceIdType.MESH,
+        )
+
+    def send_pieces(step, carry):
+        def send_piece(offset, inner):
+            piece_copy(step, (me + offset) % devices, me).start()
+            return inner
+
+        lax.fori_loop(1, devices, send_piece, 0)
+        data[step, me] = piece_ref[step, me]
+        return carry
+
+    lax.fori_loop(0, blocks, send_pieces, 0)
+
     first_chan = (radix * subs * my_stn + radix_local * my_chan).astype(jnp.float32)
 
     def phase(delay, step):
@@ -430,28 +459,6 @@
         return carry
 
     lax.fori_loop(0, beams // row_block, begin, 0)
-    pl.semaphore_wait(barrier, devices - 1)
-
-    def piece_copy(step, peer, slot):
-        return pltpu.make_async_remote_copy(
-            src_ref=piece_ref.at[step, peer],
-            dst_ref=data.at[step, slot],
-            send_sem=in_send.at[step, peer],
-            recv_sem=in_recv.at[step, slot],
-            device_id=place(peer),
-            device_id_type=pl.DeviceIdType.MESH,
-        )
-
-    def send_pieces(step, carry):
-        def send_piece(offset, inner):
-            piece_copy(step, (me + offset) % devices, me).start()
-            return inner
-
-        lax.fori_loop(1, devices, send_piece, 0)
-        data[step, me] = piece_ref[step, me]
-        return carry
-
-    lax.fori_loop(0, blocks, send_pieces, 0)
 
     def weigh(index, carry):
         spot = pl.ds(pl.multiple_of(index * row_block, row_block), row_block)
@@ -559,6 +566,26 @@
 
     lax.fori_loop(0, blocks, form, 0)
 
+    def settle_pieces(step, carry):
+        def settle(offset, inner):
+            piece_copy(step, (me + offset) % devices, me).wait_send()
+            return inner
+
+        lax.fori_loop(1, devices, settle, 0)
+        return carry
+
+    lax.fori_loop(0, blocks, settle_pieces, 0)
+
+    def settle_beams(step, carry):
+        def settle(offset, inner):
+            beam_copy(step, (my_stn + offset) % stn_groups, my_stn).wait_send()
+            return inner
+
+        lax.fori_loop(1, stn_groups, settle, 0)
+        return carry
+
+    lax.fori_loop(0, blocks, settle_beams, 0)
+
     def finish(step, carry):
         def take_beams(offset, inner):
             stn = (my_stn + offset) % stn_groups
@@ -577,26 +604,6 @@
         return carry
 
     lax.fori_loop(0, blocks, finish, 0)
-
-    def settle_pieces(step, carry):
-        def settle(offset, inner):
-            piece_copy(step, (me + offset) % devices, me).wait_send()
-            return inner
-
-        lax.fori_loop(1, devices, settle, 0)
-        return carry
-
-    lax.fori_loop(0, blocks, settle_pieces, 0)
-
-    def settle_beams(step, carry):
-        def settle(offset, inner):
-            beam_copy(step, (my_stn + offset) % stn_groups, my_stn).wait_send()
-            return inner
-
-        lax.fori_loop(1, stn_groups, settle, 0)
-        return carry
-
-    lax.fori_loop(0, blocks, settle_beams, 0)
 
 
 def fused_body(group, volts, fir, gains, delays, subsets, beam_sizes, station_ids, beam_order):

time: 46.9 us -> 42.9 us (0.915); the launches traced: 46.8 us -> 42.2 us
  Pallas kernels: 45.9 us -> 41.2 us
    pallas_call x1, Pallas kernels: 45.9 us -> 41.2 us  [fused_body(): pl.pallas_call(functools.partial(whole_kernel, (group, subs, chan_dev, gr...]
where the time goes in v2:
time: 42.9 us; the launch traced here: 42.2 us
  Pallas kernels  41.2 us (96%)
  local copies, waits for them, and re-layouts  0.91 us (2%)
    pallas_call x1, Pallas kernels, fused_body(): pl.pallas_call(functools.partial(whole_kernel, (group, subs, chan_dev, gr...  41.2 us
    unnamed x1, local copies, waits for them, and re-layouts  0.91 us

profile of v2, /device:TPU:0, one launch (start us, length us, event | category | flops | bytes accessed | tf_op | source)
XLA Modules:
  0.0 42.2 jit_solution(12921745488172168613)
XLA Ops:
  0.0 41.2 %whole.1 = bf16[2,3,576,128]{3,2,1,0:T(8,128)(2,1)S(1)} custom-call(bf16[2,19,8,3072]{3,2,1,0:T(8,128)(2,1)} %bitcast.6, f32[16,3072]{1,0:T(8,128)} %fir_in.1, f32[24,128]{1,0:T(8,128)} %constant.6.clone.cos_in, f32[24,128]{1,0:T(8,128)} %constant.7.clone.sin_in, f32[256,256]{1,0:T(8,128)} %constant.8.clone.table_in, f32[192,128]{1,0:T(8,128)} %bitcast.7, ...), custom_call_target="tpu_custom_call" | custom-call | tf_op jit(solution)/shard_map/whole/pallas_call | solution.py:649
  41.2 0.9 %copy.13 = bf16[2,12,128,18,8]{2,4,3,1,0:T(8,128)(2,1)} copy(bf16[2,12,128,18,8]{2,4,3,1,0:T(8,128)(2,1)S(1)} %bitcast.5) | data formatting | bytes 1769472
